TPU v7x, 32 devices: a whole 2x2x4 slice. The times are simulated.
32 devices in a mesh: dp: 8 (over z, x), tensor: 4 (over y, core).
Axes of the slice: x: 2, y: 2, z: 4, core: 2. Of those that a mesh axis runs over, the one named last changes fastest.
Arguments:
- features: bfloat16 [32768, 768], P(('dp', 'tensor')), may hold values from -6 to 6
- first_gain: bfloat16 [768], replicated, may hold values from 0.5 to 1.5
- first_shift: bfloat16 [768], replicated, may hold values from -2 to 2
- qkv_weight: bfloat16 [768, 3, 768], P('dp', None, 'tensor'), may hold values from -0.21875 to 0.21875
- qv_bias: bfloat16 [2, 768], P(None, 'tensor'), may hold values from -1.1953125 to 1.1953125
- rel_height: bfloat16 [27, 64], replicated, may hold values from -0.59765625 to 0.59765625
- rel_width: bfloat16 [27, 64], replicated, may hold values from -0.59765625 to 0.59765625
- output_weight: bfloat16 [768, 768], P('dp', 'tensor'), may hold values from -1.25 to 1.25
- output_bias: bfloat16 [768], replicated, may hold values from -2 to 2
- second_gain: bfloat16 [768], replicated, may hold values from 0.5 to 1.5
- second_shift: bfloat16 [768], replicated, may hold values from -2 to 2
- up_weight: bfloat16 [768, 3072], P('dp', 'tensor'), may hold values from -0.21875 to 0.21875
- up_bias: bfloat16 [3072], P('tensor'), may hold values from -2 to 2
- down_weight: bfloat16 [768, 3072], P('dp', 'tensor'), may hold values from -0.109375 to 0.109375
- down_bias: bfloat16 [768], replicated, may hold values from -2 to 2
- cotangent: bfloat16 [32768, 768], P(('dp', 'tensor')), may hold values from -6 to 6
Outputs:
- output: bfloat16 [32768, 768], P(('dp', 'tensor'))
- grad_features: bfloat16 [32768, 768], P(('dp', 'tensor'))
- grad_first_gain: float32 [768], replicated
- grad_first_shift: float32 [768], replicated
- grad_qkv_weight: float32 [768, 3, 768], P('dp', None, 'tensor')
- grad_qv_bias: float32 [2, 768], P(None, 'tensor')
- grad_rel_height: float32 [27, 64], replicated
- grad_rel_width: float32 [27, 64], replicated
- grad_output_weight: float32 [768, 768], P('dp', 'tensor')
- grad_output_bias: float32 [768], replicated
- grad_second_gain: float32 [768], replicated
- grad_second_shift: float32 [768], replicated
- grad_up_weight: float32 [768, 3072], P('dp', 'tensor')
- grad_up_bias: float32 [3072], P('tensor')
- grad_down_weight: float32 [768, 3072], P('dp', 'tensor')
- grad_down_bias: float32 [768], replicated
All inputs are finite; a program needn't handle non-finite values.
Results may differ from a plain program's by a relative error of at most 0.015.
Values may be sent and summed in bfloat16 or wider, within the bound.
No kernel may reach another device: no remote copies, remote signals or barrier semaphores. Data moves between devices by JAX's collectives and lax.ppermute only.
A program may use at most 192 MiB of HBM per device.

v0:
```python
from functools import partial
import math
import jax
import jax.numpy as jnp
from jax import lax
from jax.sharding import PartitionSpec as P

D = 768
HD = 64
GRID = 64
WIN = 14
SIDE = 5
EPSILON = 1e-06
HIGH = lax.Precision.HIGHEST


def norm_parts(value):
    mean_value = jnp.mean(value, -1, keepdims=True)
    centered = value - mean_value
    inverse_deviation = lax.rsqrt(jnp.mean(centered * centered, -1, keepdims=True) + EPSILON)
    return (centered * inverse_deviation, inverse_deviation)


def norm_backward(upstream_gradient, normalized_input, inverse_deviation, gain_factor):
    scaled_input = upstream_gradient * gain_factor
    inner_product = (
        scaled_input
        - jnp.mean(scaled_input, -1, keepdims=True)
        - normalized_input * jnp.mean(scaled_input * normalized_input, -1, keepdims=True)
    )
    return (
        inverse_deviation * inner_product,
        jnp.sum(upstream_gradient * normalized_input, 0),
        jnp.sum(upstream_gradient, 0),
    )


def to_windows(flat, images):
    width = flat.shape[-1]
    extra = SIDE * WIN - GRID
    grid = jnp.pad(
        flat.reshape(images, GRID, GRID, width), ((0, 0), (0, extra), (0, extra), (0, 0))
    )
    grid = grid.reshape(images, SIDE, WIN, SIDE, WIN, width).transpose(0, 1, 3, 2, 4, 5)
    return grid.reshape(images * SIDE * SIDE, WIN * WIN, width)


def from_windows(windows, images):
    width = windows.shape[-1]
    grid = windows.reshape(images, SIDE, SIDE, WIN, WIN, width).transpose(0, 1, 3, 2, 4, 5)
    grid = grid.reshape(images, SIDE * WIN, SIDE * WIN, width)
    return grid[:, :GRID, :GRID].reshape(images * GRID * GRID, width)


def offset_table():
    offsets = jnp.arange(WIN)[:, None] - jnp.arange(WIN)[None, :] + WIN - 1
    return (offsets[:, :, None] == jnp.arange(2 * WIN - 1)[None, None, :]).astype(jnp.float32)


def spread_table():
    places = jnp.arange(WIN * WIN)
    marks = jnp.arange(WIN)[:, None]
    row_part = places[None, :] // WIN == marks
    col_part = places[None, :] % WIN == marks
    return jnp.concatenate([row_part, col_part], 0).astype(jnp.float32)


def contract_first(left, right):
    return lax.dot_general(
        left, right, (((0,), (0,)), ((), ())), preferred_element_type=jnp.float32
    )


def contract_last(left, right):
    return lax.dot_general(
        left, right, (((1,), (1,)), ((), ())), preferred_element_type=jnp.float32
    )


def scores_of(query, keys, table_rows, table_cols, spread):
    blocks, heads = (query.shape[0], query.shape[2])
    scores = jnp.einsum(
        "nqhc,nkhc->nhqk", query, keys, preferred_element_type=jnp.float32
    ) * HD ** (-0.5)
    query_grid = query.reshape(blocks, WIN, WIN, heads, HD)
    along_rows = jnp.einsum(
        "nabhc,akc->nhabk", query_grid, table_rows, preferred_element_type=jnp.float32
    )
    along_cols = jnp.einsum(
        "nabhc,bkc->nhabk", query_grid, table_cols, preferred_element_type=jnp.float32
    )
    along = jnp.concatenate([along_rows, along_cols], -1).reshape(blocks, heads, WIN * WIN, 2 * WIN)
    return scores + jnp.einsum("nhqj,jk->nhqk", along, spread, precision=HIGH)


def attend(tables, block):
    scores = scores_of(block[:, :, 0], block[:, :, 1], tables[0], tables[1], tables[2])
    largest = jnp.max(scores, -1, keepdims=True)
    log_total = largest + jnp.log(jnp.sum(jnp.exp(scores - largest), -1, keepdims=True))
    probs = jnp.exp(scores - log_total).astype(jnp.bfloat16)
    attended = jnp.einsum(
        "nhqk,nkhc->nqhc", probs, block[:, :, 2], preferred_element_type=jnp.float32
    )
    return (attended.astype(jnp.bfloat16), log_total)


def attend_back(tables, carry, items):
    block, upstream_gradient, log_total = items
    query, keys, values = (block[:, :, 0], block[:, :, 1], block[:, :, 2])
    blocks, heads = (query.shape[0], query.shape[2])
    probs = jnp.exp(scores_of(query, keys, tables[0], tables[1], tables[2]) - log_total)
    grad_values = jnp.einsum(
        "nhqk,nqhc->nkhc",
        probs.astype(jnp.bfloat16),
        upstream_gradient,
        preferred_element_type=jnp.float32,
    )
    grad_probs = jnp.einsum(
        "nqhc,nkhc->nhqk", upstream_gradient, values, preferred_element_type=jnp.float32
    )
    grad_scores = (probs * (grad_probs - jnp.sum(probs * grad_probs, -1, keepdims=True))).astype(
        jnp.bfloat16
    )
    grad_query = jnp.einsum(
        "nhqk,nkhc->nqhc", grad_scores, keys, preferred_element_type=jnp.float32
    ) * HD ** (-0.5)
    grad_keys = jnp.einsum(
        "nhqk,nqhc->nkhc", grad_scores, query, preferred_element_type=jnp.float32
    ) * HD ** (-0.5)
    key_sums = jnp.einsum(
        "nhqk,jk->nhqj", grad_scores, tables[3], preferred_element_type=jnp.float32
    )
    key_sums = key_sums.reshape(blocks, heads, WIN, WIN, 2 * WIN)
    sum_rows = key_sums[..., :WIN]
    sum_cols = key_sums[..., WIN:]
    rows_float = tables[0].astype(jnp.float32)
    cols_float = tables[1].astype(jnp.float32)
    extra = jnp.einsum("nhabk,akc->nabhc", sum_rows, rows_float, precision=HIGH)
    extra = extra + jnp.einsum("nhabk,bkc->nabhc", sum_cols, cols_float, precision=HIGH)
    grad_query = grad_query + extra.reshape(blocks, WIN * WIN, heads, HD)
    query_float = query.astype(jnp.float32).reshape(blocks, WIN, WIN, heads, HD)
    table_grad_rows = carry[0] + jnp.einsum(
        "nhabk,nabhc->akc", sum_rows, query_float, precision=HIGH
    )
    table_grad_cols = carry[1] + jnp.einsum(
        "nhabk,nabhc->bkc", sum_cols, query_float, precision=HIGH
    )
    grads = jnp.stack([grad_query, grad_keys, grad_values], axis=2).astype(jnp.bfloat16)
    return ((table_grad_rows, table_grad_cols), grads)


def gelu_slope(upper):
    return 0.5 * (1.0 + lax.erf(upper / math.sqrt(2.0))) + upper * jnp.exp(
        -0.5 * upper * upper
    ) / math.sqrt(2.0 * math.pi)


def feed_rows(normed, up_full, up_shift, down_full):
    upper = jnp.dot(normed, up_full, preferred_element_type=jnp.float32) + up_shift
    active = jax.nn.gelu(upper, approximate=False).astype(jnp.bfloat16)
    return contract_last(active, down_full)


def feed_back_rows(normed, grads, up_full, up_shift, down_full, block):
    steps = normed.shape[0] // block
    hidden = up_full.shape[1]

    def step(carry, items):
        part_in, part_grad = items
        upper = jnp.dot(part_in, up_full, preferred_element_type=jnp.float32) + up_shift
        active = jax.nn.gelu(upper, approximate=False).astype(jnp.bfloat16)
        slope = jnp.dot(part_grad, down_full, preferred_element_type=jnp.float32)
        delta = (slope * gelu_slope(upper)).astype(jnp.bfloat16)
        grad_up = carry[0] + contract_first(part_in, delta)
        grad_down = carry[1] + contract_first(part_grad, active)
        grad_shift = carry[2] + jnp.sum(delta.astype(jnp.float32), 0)
        return ((grad_up, grad_down, grad_shift), delta)

    start_carry = (
        jnp.zeros((D, hidden), jnp.float32),
        jnp.zeros((D, hidden), jnp.float32),
        jnp.zeros((hidden,), jnp.float32),
    )
    carry, deltas = lax.scan(
        step, start_carry, (normed.reshape(steps, block, D), grads.reshape(steps, block, D))
    )
    return (deltas.reshape(steps * block, hidden), carry[0], carry[1], carry[2])


def body(
    features,
    first_gain,
    first_shift,
    qkv_weight,
    qv_bias,
    rel_height,
    rel_width,
    output_weight,
    output_bias,
    second_gain,
    second_shift,
    up_weight,
    up_bias,
    down_weight,
    down_bias,
    cotangent,
):
    qkv_full, output_full, up_full, down_full = (
        lax.all_gather(qkv_weight, "dp", axis=0, tiled=True),
        lax.all_gather(output_weight, "dp", axis=0, tiled=True),
        lax.all_gather(up_weight, "dp", axis=0, tiled=True),
        lax.all_gather(down_weight, "dp", axis=0, tiled=True),
    )
    local_width = qkv_weight.shape[2]
    heads_here = local_width // HD
    own_rows = features.shape[0]
    gain_one = first_gain.astype(jnp.float32)
    gain_two = second_gain.astype(jnp.float32)
    feature_float = features.astype(jnp.float32)
    hat_one, inverse_one = norm_parts(feature_float)
    normed_one = (hat_one * gain_one + first_shift.astype(jnp.float32)).astype(jnp.bfloat16)
    normed_all = lax.all_gather(normed_one, "tensor", axis=0, tiled=True)
    images = normed_all.shape[0] // (GRID * GRID)
    normed_windows = to_windows(normed_all, images)
    bias_float = qv_bias.astype(jnp.float32)
    bias_all = jnp.stack([bias_float[0], jnp.zeros_like(bias_float[0]), bias_float[1]]).reshape(
        3 * local_width
    )
    qkv_matrix = qkv_full.reshape(D, 3 * local_width)
    qkv = (
        jnp.dot(normed_windows.reshape(-1, D), qkv_matrix, preferred_element_type=jnp.float32)
        + bias_all
    )
    qkv = qkv.astype(jnp.bfloat16).reshape(images * SIDE, SIDE, WIN * WIN, 3, heads_here, HD)
    onehot = offset_table()
    onehot_low = onehot.astype(jnp.bfloat16)
    spread = spread_table()
    table_rows = jnp.einsum(
        "akr,rc->akc", onehot_low, rel_height, preferred_element_type=jnp.float32
    ).astype(jnp.bfloat16)
    table_cols = jnp.einsum(
        "akr,rc->akc", onehot_low, rel_width, preferred_element_type=jnp.float32
    ).astype(jnp.bfloat16)
    tables = (table_rows, table_cols, spread, spread.astype(jnp.bfloat16))
    attended, log_total = lax.map(partial(attend, tables), qkv)
    on_grid = from_windows(attended.reshape(images * SIDE * SIDE, WIN * WIN, local_width), images)
    branch = lax.psum_scatter(
        contract_last(on_grid, output_full), "tensor", scatter_dimension=0, tiled=True
    )
    branch = branch + output_bias.astype(jnp.float32)
    hidden_one = feature_float + branch
    hat_two, inverse_two = norm_parts(hidden_one)
    normed_two = (hat_two * gain_two + second_shift.astype(jnp.float32)).astype(jnp.bfloat16)
    up_shift = up_bias.astype(jnp.float32)
    normed_two_all = lax.all_gather(normed_two, "tensor", axis=0, tiled=True)
    feed = lax.psum_scatter(
        feed_rows(normed_two_all, up_full, up_shift, down_full).astype(jnp.bfloat16),
        "tensor",
        scatter_dimension=0,
        tiled=True,
    ).astype(jnp.float32)
    grads_all = lax.all_gather(cotangent, "tensor", axis=0, tiled=True)
    deltas, grad_up, grad_down, grad_up_shift = feed_back_rows(
        normed_two_all, grads_all, up_full, up_shift, down_full, own_rows
    )
    grad_normed_two = lax.psum_scatter(
        contract_last(deltas, up_full), "tensor", scatter_dimension=0, tiled=True
    )
    output = (hidden_one + feed + down_bias.astype(jnp.float32)).astype(jnp.bfloat16)
    grad_float = cotangent.astype(jnp.float32)
    grad_down_shift = jnp.sum(grad_float, 0)
    back_two, grad_gain_two, grad_shift_two = norm_backward(
        grad_normed_two, hat_two, inverse_two, gain_two
    )
    grad_hidden_one = grad_float + back_two
    grad_branch = grad_hidden_one.astype(jnp.bfloat16)
    grad_output_shift = jnp.sum(grad_branch.astype(jnp.float32), 0)
    grad_branch_all = lax.all_gather(grad_branch, "tensor", axis=0, tiled=True)
    grad_output = contract_first(grad_branch_all, on_grid)
    grad_on_grid = jnp.dot(grad_branch_all, output_full, preferred_element_type=jnp.float32).astype(
        jnp.bfloat16
    )
    grad_windows = to_windows(grad_on_grid, images).reshape(
        images * SIDE, SIDE, WIN * WIN, heads_here, HD
    )
    zero_table = jnp.zeros((WIN, WIN, HD), jnp.float32)
    table_grads, grad_qkv = lax.scan(
        partial(attend_back, tables), (zero_table, zero_table), (qkv, grad_windows, log_total)
    )
    grad_qkv = grad_qkv.reshape(images * SIDE * SIDE, WIN * WIN, 3 * local_width)
    shift_sums = jnp.sum(grad_qkv.astype(jnp.float32), (0, 1)).reshape(3, local_width)
    grad_qv_shift = jnp.stack([shift_sums[0], shift_sums[2]])
    grad_qkv_grid = from_windows(grad_qkv, images)
    grad_qkv_weight = contract_first(normed_all, grad_qkv_grid).reshape(D, 3, local_width)
    grad_normed_one = lax.psum_scatter(
        contract_last(grad_qkv_grid, qkv_matrix).astype(jnp.bfloat16),
        "tensor",
        scatter_dimension=0,
        tiled=True,
    ).astype(jnp.float32)
    grad_rel_rows = jnp.einsum("akr,akc->rc", onehot, table_grads[0], precision=HIGH)
    grad_rel_cols = jnp.einsum("akr,akc->rc", onehot, table_grads[1], precision=HIGH)
    back_one, grad_gain_one, grad_shift_one = norm_backward(
        grad_normed_one, hat_one, inverse_one, gain_one
    )
    grad_features = (grad_hidden_one + back_one).astype(jnp.bfloat16)
    grad_qkv_weight, grad_output, grad_up, grad_down = (
        lax.psum_scatter(grad_qkv_weight, "dp", scatter_dimension=0, tiled=True),
        lax.psum_scatter(grad_output, "dp", scatter_dimension=0, tiled=True),
        lax.psum_scatter(grad_up, "dp", scatter_dimension=0, tiled=True),
        lax.psum_scatter(grad_down, "dp", scatter_dimension=0, tiled=True),
    )
    (
        grad_gain_one,
        grad_shift_one,
        grad_gain_two,
        grad_shift_two,
        grad_output_shift,
        grad_down_shift,
        grad_rel_rows,
        grad_rel_cols,
    ) = lax.psum(
        (
            grad_gain_one,
            grad_shift_one,
            grad_gain_two,
            grad_shift_two,
            grad_output_shift,
            grad_down_shift,
            grad_rel_rows,
            grad_rel_cols,
        ),
        ("dp", "tensor"),
    )
    grad_qv_shift, grad_up_shift = lax.psum((grad_qv_shift, grad_up_shift), "dp")
    return (
        output,
        grad_features,
        grad_gain_one,
        grad_shift_one,
        grad_qkv_weight,
        grad_qv_shift,
        grad_rel_rows,
        grad_rel_cols,
        grad_output,
        grad_output_shift,
        grad_gain_two,
        grad_shift_two,
        grad_up,
        grad_up_shift,
        grad_down,
        grad_down_shift,
    )


def solution(mesh):
    placed = (
        P(("dp", "tensor"), None),
        P(),
        P(),
        P("dp", None, "tensor"),
        P(None, "tensor"),
        P(),
        P(),
        P("dp", "tensor"),
        P(),
        P(),
        P(),
        P("dp", "tensor"),
        P("tensor"),
        P("dp", "tensor"),
        P(),
        P(("dp", "tensor"), None),
    )
    return jax.shard_map(
        body,
        mesh=mesh,
        in_specs=placed,
        out_specs=(
            P(("dp", "tensor"), None),
            P(("dp", "tensor"), None),
            P(),
            P(),
            P("dp", None, "tensor"),
            P(None, "tensor"),
            P(),
            P(),
            P("dp", "tensor"),
            P(),
            P(),
            P(),
            P("dp", "tensor"),
            P("tensor"),
            P("dp", "tensor"),
            P(),
        ),
        check_vma=False,
    )
```

profile of v0, /device:TPU:0, one launch (start us, length us, event | category | flops | bytes accessed | tf_op | source)
XLA Modules:
  0.0 1442.1 jit_solution(18093629953301397693)
XLA Ops:
  14.9 38.8 %all_gather.25 = bf16[768,3,192]{2,1,0:T(4,128)(2,1)S(1)} all-gather(bf16[96,3,192]{2,1,0:T(4,128)(2,1)S(1)} %copy.162), channel_id=1, replica_groups=mesh['dp'=8,'tensor'=4] {'dp'}, dimensions={0}, use_global_device_ids=true | all-gather | bytes 995328 | tf_op jit(solution)/shard_map/all_gather | solution.py:209
  55.4 33.1 %all_gather.26 = bf16[768,192]{1,0:T(8,128)(2,1)} all-gather(bf16[96,192]{1,0:T(8,128)(2,1)S(1)} %copy-done.48), channel_id=1, replica_groups=mesh['dp'=8,'tensor'=4] {'dp'}, dimensions={0}, use_global_device_ids=true | all-gather | bytes 331776 | tf_op jit(solution)/shard_map/all_gather | solution.py:210
  89.0 6.5 pad.8
  95.5 11.5 reshape.269
  107.0 7.8 copy.161
  114.8 12.2 reshape_reshape.12
  127.0 9.8 add_convert_fusion
  136.8 17.7 %reshape.271 = bf16[5,5,196,3,3,64]{2,1,0,5,4,3:T(8,128)(2,1)} reshape(bf16[4900,576]{0,1:T(8,128)(2,1)} %add_convert_fusion) | data formatting | bytes 11289600 | tf_op jit(solution)/shard_map/reshape | solution.py:234
  154.5 9.7 copy.164
  164.1 62.1 %while.44 = (s32[]{:T(128)}, bf16[5,5,196,3,64]{2,4,3,1,0:T(8,128)(2,1)}, f32[5,5,3,196,1]{3,2,1,4,0:T(4,128)}, bf16[5,5,196,3,3,64]{2,5,4,1,3,0:T(8,128)(2,1)},...) while((s32[]{:T(128)}, ...), condition=%wide.region_5.6_spmd, body=%wide.region_2.5_spmd.sunk | while | flops 355972256 | bytes 23991828 | solution.py:245
  226.2 8.9 copy.165
  235.1 9.3 reshape_reshape.13
  246.2 3.9 reshape.272
  251.9 6.3 fusion.247
  260.1 96.8 %reduce-scatter.9.cloned.1.call-done = f32[1024,768]{1,0:T(8,128)} async-done(((f32[4096,768]{1,0:T(8,128)}), f32[1024,768]{1,0:T(8,128)}) %reduce-scatter.9.cloned.1.call-update) | async-done | bytes 3145744 | tf_op jit(solution)/shard_map/reduce_scatter | solution.py:247
  363.5 26.8 %all-gather.15.cloned.1.call-done = bf16[4096,768]{1,0:T(8,128)(2,1)} async-done(((bf16[1024,768]{1,0:T(8,128)(2,1)}), bf16[4096,768]{1,0:T(8,128)(2,1)}) %all-gather.15.cloned.1.call-update) | async-done | bytes 6291472 | tf_op jit(solution)/shard_map/all_gather | solution.py:262
  390.2 48.4 %all-gather.9.cloned.1.call-done = bf16[4096,768]{1,0:T(8,128)(2,1)} async-done(((bf16[1024,768]{1,0:T(8,128)(2,1)}), bf16[4096,768]{1,0:T(8,128)(2,1)}) %all-gather.9.cloned.1.call-update) | async-done | bytes 6291472 | tf_op jit(solution)/shard_map/all_gather | solution.py:255
  438.7 101.8 %while.45 = (s32[]{:T(128)}, f32[768,768]{1,0:T(8,128)}, f32[768,768]{1,0:T(8,128)}, f32[768]{0:T(1024)S(1)}, bf16[4,1024,768]{2,1,0:T(8,128)(2,1)}, /*index=5*/...) while((s32[]{:T(128)}, f32[768,768]{1,0:T(8,128)}, ...), condition=%wide.region_12.13_spmd.clone, body=%wide.region_10.12_spmd.clone.sunk | while | flops 4896326144 | bytes 63722192 | solution.py:184
  442.1 5.3 convert_reduce_fusion.7
  448.8 4.5 select_add_fusion.6
  453.3 10.3 select_add_fusion.7
  466.8 5.3 convert_reduce_fusion.7
  473.5 5.2 select_add_fusion.6
  478.7 10.5 select_add_fusion.7
  492.5 5.3 convert_reduce_fusion.7
  499.1 5.2 select_add_fusion.6
  504.3 10.5 select_add_fusion.7
  518.1 5.3 convert_reduce_fusion.7
  524.7 5.2 select_add_fusion.6
  529.9 10.5 select_add_fusion.7
  540.4 10.1 fusion.248
  552.2 38.3 %convolution_convert_fusion.1 = bf16[4096,768]{1,0:T(8,128)(2,1)} fusion(bf16[768,768]{1,0:T(8,128)(2,1)S(1)} %copy-done.63, f32[768]{0:T(1024)S(1)} %get-tuple-element.757, bf16[4096,768]{1,0:T(8,128)(2,1)} %bitcast.323, bf16[768,768]{1,0:T(8,128)(2,1)S(1)} %copy-done.61), kind=kOutput, calls=%fused_computation.213 | convolution fusion | flops 9874440192 | bytes 14945280 | tf_op jit(solution)/shard_map/dot_general | solution.py:75
  591.2 58.4 %reduce-scatter.13.cloned.1.call-done = f32[1024,768]{1,0:T(8,128)} async-done(((f32[4096,768]{1,0:T(8,128)}), f32[1024,768]{1,0:T(8,128)}) %reduce-scatter.13.cloned.1.call-update) | async-done | bytes 3145744 | tf_op jit(solution)/shard_map/reduce_scatter | solution.py:266
  649.7 3.7 multiply_reduce_fusion.1
  653.3 57.1 %reduce-scatter.11.cloned.1.call-done = bf16[1024,768]{1,0:T(8,128)(2,1)} async-done(((bf16[4096,768]{1,0:T(8,128)(2,1)}), bf16[1024,768]{1,0:T(8,128)(2,1)}) %reduce-scatter.11.cloned.1.call-update) | async-done | bytes 1572880 | tf_op jit(solution)/shard_map/reduce_scatter | solution.py:256
  710.5 6.1 convert_reduce_fusion.5
  716.6 46.5 %all-gather.17.cloned.1.call-done = bf16[4096,768]{1,0:T(8,128)(2,1)} async-done(((bf16[1024,768]{1,0:T(8,128)(2,1)}), bf16[4096,768]{1,0:T(8,128)(2,1)}) %all-gather.17.cloned.1.call-update) | async-done | bytes 6291472 | tf_op jit(solution)/shard_map/all_gather | solution.py:278
  763.1 5.1 convolution_convert_fusion.2
  777.9 5.3 reshape_reshape.14
  783.2 8.5 copy.170
  791.7 223.9 %while.46 = (s32[]{:T(128)}, f32[14,14,64]{2,1,0:T(8,128)S(1)}, f32[14,14,64]{2,1,0:T(8,128)S(1)}, bf16[5,5,196,3,3,64]{2,5,4,1,3,0:T(8,128)(2,1)}, bf16[5,5,196...) while((s32[]{:T(128)}, f32[14,14,64]{2,1,0:T(8,128)S(1)}, ...), condition=%wide.region_18.19_spmd.clone, body=%wide.region_16.18_spmd.clone.sunk | while | flops 741679872 | bytes 70086392 | solution.py:287
  802.8 3.4 multiply_reduce_fusion.6
  847.6 3.4 multiply_reduce_fusion.6
  892.2 3.4 multiply_reduce_fusion.6
  921.1 3.4 fusion.373
  937.0 3.4 multiply_reduce_fusion.6
  981.7 3.4 multiply_reduce_fusion.6
  1015.6 20.7 %copy.171 = bf16[5,5,196,3,3,64]{5,4,3,2,1,0:T(4,128)(2,1)} copy(bf16[5,5,196,3,3,64]{2,5,4,1,3,0:T(8,128)(2,1)} %get-tuple-element.171) | data formatting | bytes 11289600 | tf_op jit(solution)/shard_map/while | solution.py:287
  1036.3 26.7 %reshape_reshape.15 = bf16[1,5,5,14,14,576]{5,4,3,2,1,0:T(8,128)(2,1)} reshape(bf16[5,5,196,3,3,64]{5,4,3,2,1,0:T(4,128)(2,1)} %copy.171) | data formatting | bytes 11289600 | tf_op jit(solution)/shard_map/reshape;reshape | solution.py:50
  1063.0 6.5 copy.172
  1069.4 10.7 reshape.279
  1085.4 6.9 convolution_convert_fusion
  1093.6 8.0 copy.173
  1101.6 6.4 fusion.249
  1108.1 9.7 fusion.182
  1117.9 4.5 convert_reduce_fusion.1
  1122.6 22.5 %all-reduce.3 = (f32[2,192]{1,0:T(2,128)}, f32[768]{0:T(1024)}) all-reduce(f32[2,192]{1,0:T(2,128)S(1)} %pad_maximum_fusion.3, f32[768]{0:T(1024)S(1)} %copy-done.32), channel_id=1, replica_groups=mesh['dp'=8,'tensor'=4] {'dp'}, use_global_device_ids=true, to_apply=%region_28.29 | all-reduce | flops 1152 | bytes 9216 | tf_op jit(solution)/shard_map/psum | solution.py:335
  1145.7 5.2 reduce-scatter.15.cloned.1.call-done
  1154.0 41.7 %all-reduce.2 = (f32[768]{0:T(1024)}, f32[768]{0:T(1024)}, f32[27,64]{1,0:T(8,128)}, f32[27,64]{1,0:T(8,128)}, f32[768]{0:T(1024)}, /*index=5*/f32[768]{0:T(1024)}, f32[768]{0:T(1024)}, f32[768]{0:T(1024)}) all-reduce(f32[768]{0:T(1024)S(1)} %get-tuple-element.320, ...), channel_id=1, replica_groups=mesh['dp'=8,'tensor'=4] {'dp','tensor'}, use_global_device_ids=true, to_apply=%region_23.24 | all-reduce | flops 8064 | bytes 64512 | tf_op jit(solution)/shard_map/psum | solution.py:322
  1195.7 3.6 fusion.199
  1199.4 25.2 %reduce-scatter.21.cloned.1.call-done = f32[96,768]{1,0:T(8,128)} async-done(((f32[768,768]{1,0:T(8,128)}), f32[96,768]{1,0:T(8,128)}) %reduce-scatter.21.cloned.1.call-update) | async-done | bytes 294928 | tf_op jit(solution)/shard_map/reduce_scatter | solution.py:310
  1224.6 72.0 %reduce-scatter.23.cloned.1.call-done = f32[96,768]{1,0:T(8,128)} async-done(((f32[768,768]{1,0:T(8,128)}), f32[96,768]{1,0:T(8,128)}) %reduce-scatter.23.cloned.1.call-update) | async-done | bytes 294928 | tf_op jit(solution)/shard_map/reduce_scatter | solution.py:311
  1296.5 65.3 %reduce-scatter.19.cloned.1.call-done = f32[96,192]{1,0:T(8,128)} async-done(((f32[768,192]{1,0:T(8,128)}), f32[96,192]{1,0:T(8,128)}) %reduce-scatter.19.cloned.1.call-update) | async-done | bytes 73744 | tf_op jit(solution)/shard_map/reduce_scatter | solution.py:309
  1361.9 72.4 %reduce-scatter.17.cloned.1.call-done = f32[96,3,192]{2,0,1:T(8,128)} async-done(((f32[768,3,192]{2,0,1:T(8,128)}), f32[96,3,192]{2,0,1:T(8,128)}) %reduce-scatter.17.cloned.1.call-update) | async-done | bytes 221200 | tf_op jit(solution)/shard_map/reduce_scatter | solution.py:308
  (546 shorter events, 324.9 us)
Async XLA Ops:
  8.0 80.5 %copy-start = (bf16[27,64]{1,0:T(8,128)(2,1)S(1)}, bf16[27,64]{1,0:T(8,128)(2,1)}, u32[]{:S(2)}) copy-start(bf16[27,64]{1,0:T(8,128)(2,1)} %param.28) | copy-start | bytes 10372
  8.1 80.9 %all-gather.7.cloned.1.call-start = ((), (), s32[]{:S(2)}) async-start(), calls=%async_computation.8 | async-start | bytes 7864320 | tf_op jit(solution)/shard_map/all_gather | solution.py:222
  9.9 4.8 copy-start.33
  14.4 41.0 %copy-start.48 = (bf16[96,192]{1,0:T(8,128)(2,1)S(1)}, bf16[96,192]{1,0:T(8,128)(2,1)}, u32[]{:S(2)}) copy-start(bf16[96,192]{1,0:T(8,128)(2,1)} %param.29) | copy-start | bytes 110596
  14.4 74.3 %copy-start.64 = (bf16[27,64]{1,0:T(8,128)(2,1)S(1)}, bf16[27,64]{1,0:T(8,128)(2,1)}, u32[]{:S(2)}) copy-start(bf16[27,64]{1,0:T(8,128)(2,1)} %param.27) | copy-start | bytes 10372
  14.5 342.4 %reduce-scatter.9.cloned.1.call-start = ((), (), s32[]{:S(2)}) async-start(), calls=%async_computation.9 | async-start | bytes 15728640 | tf_op jit(solution)/shard_map/reduce_scatter | solution.py:247
  54.6 72.4 %copy-start.28 = (bf16[768,3,192]{0,2,1:T(8,128)(2,1)}, bf16[768,3,192]{0,2,1:T(8,128)(2,1)S(1)}, u32[]{:S(2)}) copy-start(bf16[768,3,192]{0,2,1:T(8,128)(2,1)S(1)} %copy.163) | copy-start | bytes 2654212
  54.7 40.8 %copy-start.38 = (s32[14,14]{1,0:T(8,128)}, s32[14,14]{1,0:T(8,128)S(1)}, u32[]{:S(2)}) copy-start(s32[14,14]{1,0:T(8,128)S(1)} %subtract_add_fusion) | copy-start | bytes 2356
  226.2 8.9 copy-start.20
  226.2 8.9 copy-start.22
  226.2 8.9 copy-start.25
  258.2 98.7 %copy-start.15 = (bf16[1024,768]{1,0:T(8,128)(2,1)S(1)}, bf16[1024,768]{1,0:T(8,128)(2,1)}, u32[]{:S(2)}) copy-start(bf16[1024,768]{1,0:T(8,128)(2,1)} %param.22) | copy-start | bytes 4718596
  258.2 105.2 %all-gather.11.cloned.1.call-start = ((), (), s32[]{:S(2)}) async-start(), calls=%async_computation.11 | async-start | bytes 1327104 | tf_op jit(solution)/shard_map/all_gather | solution.py:211
  258.8 104.7 %all-gather.13.cloned.1.call-start = ((), (), s32[]{:S(2)}) async-start(), calls=%async_computation.12 | async-start | bytes 1327104 | tf_op jit(solution)/shard_map/all_gather | solution.py:212
  259.4 130.9 %all-gather.15.cloned.1.call-start = ((), (), s32[]{:S(2)}) async-start(), calls=%async_computation.14 | async-start | bytes 7864320 | tf_op jit(solution)/shard_map/all_gather | solution.py:262
  259.9 178.7 %all-gather.9.cloned.1.call-start = ((), (), s32[]{:S(2)}) async-start(), calls=%async_computation.10 | async-start | bytes 7864320 | tf_op jit(solution)/shard_map/all_gather | solution.py:255
  260.0 99.8 %copy-start.44 = (f32[768]{0:T(1024)}, f32[768]{0:T(1024)S(1)}, u32[]{:S(2)}) copy-start(f32[768]{0:T(1024)S(1)} %convert_element_type.146) | copy-start | bytes 9220
  363.3 286.4 %reduce-scatter.13.cloned.1.call-start = ((), (), s32[]{:S(2)}) async-start(), calls=%async_computation.15 | async-start | bytes 15728640 | tf_op jit(solution)/shard_map/reduce_scatter | solution.py:266
  442.1 5.4 copy-start.65
  466.8 5.4 copy-start.65
  473.5 5.2 copy-start.66
  492.4 5.4 copy-start.65
  499.1 5.2 copy-start.66
  518.1 5.4 copy-start.65
  524.7 5.2 copy-start.66
  540.4 10.1 copy-start.31
  550.6 159.9 %reduce-scatter.11.cloned.1.call-start = ((), (), s32[]{:S(2)}) async-start(), calls=%async_computation.13 | async-start | bytes 7864320 | tf_op jit(solution)/shard_map/reduce_scatter | solution.py:256
  590.5 59.1 %copy-start.13 = (f32[1024,768]{1,0:T(8,128)S(1)}, f32[1024,768]{1,0:T(8,128)}, u32[]{:S(2)}) copy-start(f32[1024,768]{1,0:T(8,128)} %copy-done.12) | copy-start | bytes 9437188
  590.5 59.1 %copy-start.37 = (f32[1024]{0:T(1024)S(1)}, f32[1024]{0:T(1024)}, u32[]{:S(2)}) copy-start(f32[1024]{0:T(1024)} %copy-done.36) | copy-start | bytes 12292
  590.5 59.1 %copy-start.45 = (f32[768]{0:T(1024)S(1)}, f32[768]{0:T(1024)}, u32[]{:S(2)}) copy-start(f32[768]{0:T(1024)} %copy-done.44) | copy-start | bytes 9220
  590.5 59.1 %copy-start.47 = (f32[1024]{0:T(1024)S(1)}, f32[1024]{0:T(1024)}, u32[]{:S(2)}) copy-start(f32[1024]{0:T(1024)} %copy-done.46) | copy-start | bytes 12292
  590.6 172.5 %all-gather.17.cloned.1.call-start = ((), (), s32[]{:S(2)}) async-start(), calls=%async_computation.16 | async-start | bytes 7864320 | tf_op jit(solution)/shard_map/all_gather | solution.py:278
  716.5 434.4 %reduce-scatter.15.cloned.1.call-start = ((), (), s32[]{:S(2)}) async-start(), calls=%async_computation.17 | async-start | bytes 7864320 | tf_op jit(solution)/shard_map/reduce_scatter | solution.py:295
  783.1 8.5 copy-start.21
  783.1 8.5 copy-start.23
  783.1 8.5 copy-start.26
  783.2 8.5 copy-start.30
  793.3 8.1 copy-start.9
  830.2 4.9 copy-start.7
  838.1 8.1 copy-start.9
  874.9 4.8 copy-start.7
  882.8 8.1 copy-start.9
  919.6 4.9 copy-start.7
  927.5 8.1 copy-start.9
  964.3 4.8 copy-start.7
  972.2 8.1 copy-start.9
  1009.0 4.9 copy-start.7
  1080.1 5.3 copy-start.29
  1092.4 132.1 %reduce-scatter.21.cloned.1.call-start = ((), (), s32[]{:S(2)}) async-start(), calls=%async_computation.20 | async-start | bytes 2654208 | tf_op jit(solution)/shard_map/reduce_scatter | solution.py:310
  1093.0 203.5 %reduce-scatter.23.cloned.1.call-start = ((), (), s32[]{:S(2)}) async-start(), calls=%async_computation.21 | async-start | bytes 2654208 | tf_op jit(solution)/shard_map/reduce_scatter | solution.py:311
  1093.6 268.3 %reduce-scatter.19.cloned.1.call-start = ((), (), s32[]{:S(2)}) async-start(), calls=%async_computation.19 | async-start | bytes 884736 | tf_op jit(solution)/shard_map/reduce_scatter | solution.py:309
  1093.6 8.0 copy-start.18
  1108.0 326.2 %reduce-scatter.17.cloned.1.call-start = ((), (), s32[]{:S(2)}) async-start(), calls=%async_computation.18 | async-start | bytes 2654208 | tf_op jit(solution)/shard_map/reduce_scatter | solution.py:308
  1117.8 27.2 %copy-start.39 = (s32[14,14]{1,0:T(8,128)S(1)}, s32[14,14]{1,0:T(8,128)}, u32[]{:S(2)}) copy-start(s32[14,14]{1,0:T(8,128)} %copy-done.38) | copy-start | bytes 2356
  1117.8 33.1 %copy-start.16 = (bf16[1024,768]{1,0:T(8,128)(2,1)S(1)}, bf16[1024,768]{1,0:T(8,128)(2,1)}, u32[]{:S(2)}) copy-start(bf16[1024,768]{1,0:T(8,128)(2,1)} %param.22) | copy-start | bytes 4718596
  1117.8 33.1 %copy-start.35 = (f32[1024]{0:T(1024)S(1)}, f32[1024]{0:T(1024)}, u32[]{:S(2)}) copy-start(f32[1024]{0:T(1024)} %copy-done.34) | copy-start | bytes 12292
  1117.8 33.1 %copy-start.41 = (f32[1024]{0:T(1024)S(1)}, f32[1024]{0:T(1024)}, u32[]{:S(2)}) copy-start(f32[1024]{0:T(1024)} %copy-done.40) | copy-start | bytes 12292
  1117.8 33.1 %copy-start.43 = (f32[768]{0:T(1024)S(1)}, f32[768]{0:T(1024)}, u32[]{:S(2)}) copy-start(f32[768]{0:T(1024)} %copy-done.42) | copy-start | bytes 9220
  1122.4 31.7 %copy-start.49 = (f32[768]{0:T(1024)S(1)}, f32[768]{0:T(1024)}, u32[]{:S(2)}) copy-start(f32[768]{0:T(1024)} %get-tuple-element.318) | copy-start | bytes 9220
  1122.4 31.7 %copy-start.50 = (f32[768]{0:T(1024)S(1)}, f32[768]{0:T(1024)}, u32[]{:S(2)}) copy-start(f32[768]{0:T(1024)} %get-tuple-element.323) | copy-start | bytes 9220
  1122.4 31.7 %copy-start.51 = (f32[768]{0:T(1024)S(1)}, f32[768]{0:T(1024)}, u32[]{:S(2)}) copy-start(f32[768]{0:T(1024)} %get-tuple-element.394) | copy-start | bytes 9220
  1122.4 31.7 %copy-start.52 = (f32[768]{0:T(1024)S(1)}, f32[768]{0:T(1024)}, u32[]{:S(2)}) copy-start(f32[768]{0:T(1024)} %get-tuple-element.408) | copy-start | bytes 9220
  1150.9 44.8 %copy-start.24 = (bf16[1024,768]{1,0:T(8,128)(2,1)S(1)}, bf16[1024,768]{1,0:T(8,128)(2,1)}, u32[]{:S(2)}) copy-start(bf16[1024,768]{1,0:T(8,128)(2,1)} %reduce-scatter.15.cloned.1.call-done) | copy-start | bytes 4718596
  1195.7 238.5 %copy-start.1 = (bf16[27,64]{1,0:T(8,128)(2,1)S(1)}, bf16[27,64]{1,0:T(8,128)(2,1)}, u32[]{:S(2)}) copy-start(bf16[27,64]{1,0:T(8,128)(2,1)} %param.28) | copy-start | bytes 10372
  (66 other events, 148.1 us)
Sparse Core Ops, SparseCore 0:
  14.6 49.0 all-gather.6
  258.3 98.4 reduce-scatter.8
  716.7 46.3 all-gather.16
  1092.5 58.3 reduce-scatter.14
  1154.8 69.6 reduce-scatter.20
  1228.5 68.0 reduce-scatter.22
  1300.4 61.4 reduce-scatter.18
  1366.3 67.8 reduce-scatter.16
Sparse Core Ops, SparseCore 1:
  260.9 40.6 all-gather.10
  303.6 39.8 all-gather.12
  344.9 45.3 all-gather.14
  392.4 46.2 all-gather.8
  550.7 98.9 reduce-scatter.12
  652.2 58.2 reduce-scatter.10
where the time goes:
time: 1460 us; the launch traced here: 1440 us
  waiting for transfers between devices  577 us (40%)
  local copies, waits for them, and re-layouts  329 us (23%)
  matrix products  328 us (22%)
  blocking collectives  136 us (9%)
  other arithmetic  53.1 us (4%)
  between operations  16.8 us (1%)
    reduce_scatter x1, waiting for transfers between devices, body(): lax.psum_scatter(contract_last(on_grid, output_full), 'tensor', scatter_d...  96.8 us
    dot_general x10, matrix products, contract_first(): lax.dot_general(left, right, (((0,), (0,)), ((), ())), preferred_element_...  78 us
    reduce_scatter x1, waiting for transfers between devices, body(): lax.psum_scatter(grad_qkv_weight, 'dp', scatter_dimension=0, tiled=True)  72.4 us
    reduce_scatter x1, waiting for transfers between devices, body(): lax.psum_scatter(grad_down, 'dp', scatter_dimension=0, tiled=True)  72 us
    reduce_scatter x1, waiting for transfers between devices, body(): lax.psum_scatter(grad_output, 'dp', scatter_dimension=0, tiled=True)  65.3 us
    dot_general x4, matrix products, contract_last(): lax.dot_general(left, right, (((1,), (1,)), ((), ())), preferred_element_...  61.7 us
    reduce_scatter x1, waiting for transfers between devices, body(): lax.psum_scatter(contract_last(deltas, up_full), 'tensor', scatter_dimens...  58.4 us
    reduce_scatter x1, waiting for transfers between devices, body(): lax.psum_scatter(feed_rows(normed_two_all, up_full, up_shift, down_full)....  57.1 us
  transfers between devices with their start and end apart: 14, of which 11 were waited for; matrix products, arithmetic and copies ran while one was open for 6% of the time, Pallas kernels for 0%

commit v1 on v0

--- a/solution.py
+++ b/solution.py
@@ -252,7 +252,14 @@
     hat_two, inverse_two = norm_parts(hidden_one)
     normed_two = (hat_two * gain_two + second_shift.astype(jnp.float32)).astype(jnp.bfloat16)
     up_shift = up_bias.astype(jnp.float32)
-    normed_two_all = lax.all_gather(normed_two, "tensor", axis=0, tiled=True)
+    devices = lax.axis_size("tensor")
+    route = [(i, (i + 1) % devices) for i in range(devices)]
+    parts = [normed_two]
+    for far in range(1, devices):
+        parts = [lax.ppermute(parts[0], "tensor", route), *parts]
+    whole = jnp.concatenate(parts, axis=0)
+    shift = (lax.axis_index("tensor") + 1) * parts[-1].shape[0]
+    normed_two_all = jnp.roll(whole, shift, axis=0)
     feed = lax.psum_scatter(
         feed_rows(normed_two_all, up_full, up_shift, down_full).astype(jnp.bfloat16),
         "tensor",

time: 1460 us -> 1470 us (level)
    ppermute x0 -> x3, waiting for transfers between devices: none -> 84.5 us  [body(): parts = [lax.ppermute(parts[0], 'tensor', route), *parts]]
    all_gather x1 -> x0, waiting for transfers between devices: 48.4 us -> none  [body(): normed_two_all = lax.all_gather(normed_two, 'tensor', axis=0, tiled=True)]
    all_gather x1, waiting for transfers between devices: 26.8 us -> 0.01 us  [body(): grads_all = lax.all_gather(cotangent, 'tensor', axis=0, tiled=True)]
  transfers between devices with their start and end apart: 14 -> 16, of which waited for: 11 -> 12; matrix products, arithmetic and copies ran while one was open for 6% -> 6% of each run, Pallas kernels for 0% -> 0%
where the time goes in v1:
time: 1470 us; the launch traced here: 1460 us
  waiting for transfers between devices  587 us (40%)
  local copies, waits for them, and re-layouts  337 us (23%)
  matrix products  327 us (22%)
  blocking collectives  136 us (9%)
  other arithmetic  53.5 us (4%)
  between operations  16.9 us (1%)
    reduce_scatter x1, waiting for transfers between devices, body(): lax.psum_scatter(contract_last(on_grid, output_full), 'tensor', scatter_d...  96.7 us
    ppermute x3, waiting for transfers between devices, body(): parts = [lax.ppermute(parts[0], 'tensor', route), *parts]  84.5 us
    dot_general x10, matrix products, contract_first(): lax.dot_general(left, right, (((0,), (0,)), ((), ())), preferred_element_...  78.2 us
    reduce_scatter x1, waiting for transfers between devices, body(): lax.psum_scatter(grad_qkv_weight, 'dp', scatter_dimension=0, tiled=True)  72.4 us
    reduce_scatter x1, waiting for transfers between devices, body(): lax.psum_scatter(grad_down, 'dp', scatter_dimension=0, tiled=True)  72 us
    reduce_scatter x1, waiting for transfers between devices, body(): lax.psum_scatter(grad_output, 'dp', scatter_dimension=0, tiled=True)  65.4 us
    dot_general x4, matrix products, contract_last(): lax.dot_general(left, right, (((1,), (1,)), ((), ())), preferred_element_...  61.3 us
    reduce_scatter x1, waiting for transfers between devices, body(): lax.psum_scatter(contract_last(deltas, up_full), 'tensor', scatter_dimens...  59 us
  transfers between devices with their start and end apart: 16, of which 12 were waited for; matrix products, arithmetic and copies ran while one was open for 6% of the time, Pallas kernels for 0%

profile of v1, /device:TPU:0, one launch (start us, length us, event | category | flops | bytes accessed | tf_op | source)
XLA Modules:
  0.0 1461.3 jit_solution(17425841195687642743)
XLA Ops:
  14.9 38.8 %all_gather.22 = bf16[768,3,192]{2,1,0:T(4,128)(2,1)S(1)} all-gather(bf16[96,3,192]{2,1,0:T(4,128)(2,1)S(1)} %copy.162), channel_id=1, replica_groups=mesh['dp'=8,'tensor'=4] {'dp'}, dimensions={0}, use_global_device_ids=true | all-gather | bytes 995328 | tf_op jit(solution)/shard_map/all_gather | solution.py:209
  55.4 33.1 %all_gather.23 = bf16[768,192]{1,0:T(8,128)(2,1)} all-gather(bf16[96,192]{1,0:T(8,128)(2,1)S(1)} %copy-done.49), channel_id=1, replica_groups=mesh['dp'=8,'tensor'=4] {'dp'}, dimensions={0}, use_global_device_ids=true | all-gather | bytes 331776 | tf_op jit(solution)/shard_map/all_gather | solution.py:210
  89.0 6.5 pad.8
  95.5 11.5 reshape.269
  107.0 7.8 copy.161
  114.7 12.2 reshape_reshape.12
  126.9 9.8 add_convert_fusion
  136.7 17.7 %reshape.271 = bf16[5,5,196,3,3,64]{2,1,0,5,4,3:T(8,128)(2,1)} reshape(bf16[4900,576]{0,1:T(8,128)(2,1)} %add_convert_fusion) | data formatting | bytes 11289600 | tf_op jit(solution)/shard_map/reshape | solution.py:234
  154.4 9.7 copy.164
  164.1 62.1 %while.44 = (s32[]{:T(128)}, bf16[5,5,196,3,64]{2,4,3,1,0:T(8,128)(2,1)}, f32[5,5,3,196,1]{3,2,1,4,0:T(4,128)}, bf16[5,5,196,3,3,64]{2,5,4,1,3,0:T(8,128)(2,1)},...) while((s32[]{:T(128)}, ...), condition=%wide.region_5.6_spmd, body=%wide.region_2.5_spmd.sunk | while | flops 355972256 | bytes 23991828 | solution.py:245
  226.2 8.9 copy.165
  235.1 9.3 reshape_reshape.13
  246.3 3.9 reshape.272
  251.9 6.3 fusion.247
  260.1 96.7 %reduce-scatter.9.cloned.1.call-done = f32[1024,768]{1,0:T(8,128)} async-done(((f32[4096,768]{1,0:T(8,128)}), f32[1024,768]{1,0:T(8,128)}) %reduce-scatter.9.cloned.1.call-update) | async-done | bytes 3145744 | tf_op jit(solution)/shard_map/reduce_scatter | solution.py:247
  360.9 44.6 %collective-permute-done = bf16[1024,768]{1,0:T(8,128)(2,1)S(1)} collective-permute-done((bf16[1024,768]{1,0:T(8,128)(2,1)S(1)}, bf16[1024,768]{1,0:T(8,128)(2,1)S(1)}, u32[]{:S(2)}, u32[]{:S(2)}) %collective-permute-start) | collective-permute-done | bytes 1572896 | tf_op jit(solution)/shard_map/ppermute | solution.py:259
  406.6 19.9 %collective-permute-done.1 = bf16[1024,768]{1,0:T(8,128)(2,1)} collective-permute-done((bf16[1024,768]{1,0:T(8,128)(2,1)S(1)}, bf16[1024,768]{1,0:T(8,128)(2,1)}, u32[]{:S(2)}, u32[]{:S(2)}) %collective-permute-start.1) | collective-permute-done | bytes 1572896 | tf_op jit(solution)/shard_map/ppermute | solution.py:259
  427.0 20.0 %collective-permute-done.2 = bf16[1024,768]{1,0:T(8,128)(2,1)} collective-permute-done((bf16[1024,768]{1,0:T(8,128)(2,1)}, bf16[1024,768]{1,0:T(8,128)(2,1)}, u32[]{:S(2)}, u32[]{:S(2)}) %collective-permute-start.2) | collective-permute-done | bytes 1572896 | tf_op jit(solution)/shard_map/ppermute | solution.py:259
  457.5 101.7 %while.45 = (s32[]{:T(128)}, f32[768,768]{1,0:T(8,128)}, f32[768,768]{1,0:T(8,128)}, f32[768]{0:T(1024)S(1)}, bf16[4,1024,768]{2,1,0:T(8,128)(2,1)}, /*index=5*/...) while((s32[]{:T(128)}, f32[768,768]{1,0:T(8,128)}, ...), condition=%wide.region_12.13_spmd.clone, body=%wide.region_10.12_spmd.clone.sunk | while | flops 4896326144 | bytes 63722192 | solution.py:184
  460.8 5.3 convert_reduce_fusion.7
  467.4 4.5 select_add_fusion.6
  471.9 10.3 select_add_fusion.7
  485.5 5.3 convert_reduce_fusion.7
  492.2 5.2 select_add_fusion.6
  497.4 10.6 select_add_fusion.7
  511.2 5.3 convert_reduce_fusion.7
  517.8 5.2 select_add_fusion.6
  523.0 10.6 select_add_fusion.7
  536.9 5.3 convert_reduce_fusion.7
  543.5 5.2 select_add_fusion.6
  548.7 10.6 select_add_fusion.7
  559.3 10.2 fusion.248
  571.1 37.8 %convolution_convert_fusion.1 = bf16[4096,768]{1,0:T(8,128)(2,1)} fusion(bf16[768,768]{1,0:T(8,128)(2,1)S(1)} %copy-done.64, f32[768]{0:T(1024)S(1)} %get-tuple-element.758, bf16[4096,768]{1,0:T(8,128)(2,1)} %bitcast.319, bf16[768,768]{1,0:T(8,128)(2,1)S(1)} %copy-done.62), kind=kOutput, calls=%fused_computation.213 | convolution fusion | flops 9874440192 | bytes 14945280 | tf_op jit(solution)/shard_map/dot_general | solution.py:75
  609.6 59.0 %reduce-scatter.13.cloned.1.call-done = f32[1024,768]{1,0:T(8,128)} async-done(((f32[4096,768]{1,0:T(8,128)}), f32[1024,768]{1,0:T(8,128)}) %reduce-scatter.13.cloned.1.call-update) | async-done | bytes 3145744 | tf_op jit(solution)/shard_map/reduce_scatter | solution.py:273
  668.6 3.7 multiply_reduce_fusion.1
  672.3 57.1 %reduce-scatter.11.cloned.1.call-done = bf16[1024,768]{1,0:T(8,128)(2,1)} async-done(((bf16[4096,768]{1,0:T(8,128)(2,1)}), bf16[1024,768]{1,0:T(8,128)(2,1)}) %reduce-scatter.11.cloned.1.call-update) | async-done | bytes 1572880 | tf_op jit(solution)/shard_map/reduce_scatter | solution.py:263
  729.4 6.1 convert_reduce_fusion.5
  735.6 46.5 %all-gather.14.cloned.1.call-done = bf16[4096,768]{1,0:T(8,128)(2,1)} async-done(((bf16[1024,768]{1,0:T(8,128)(2,1)}), bf16[4096,768]{1,0:T(8,128)(2,1)}) %all-gather.14.cloned.1.call-update) | async-done | bytes 6291472 | tf_op jit(solution)/shard_map/all_gather | solution.py:285
  782.0 5.1 convolution_convert_fusion.2
  796.8 5.2 reshape_reshape.14
  802.1 8.5 copy.170
  810.6 224.2 %while.46 = (s32[]{:T(128)}, f32[14,14,64]{2,1,0:T(8,128)S(1)}, f32[14,14,64]{2,1,0:T(8,128)S(1)}, bf16[5,5,196,3,3,64]{2,5,4,1,3,0:T(8,128)(2,1)}, bf16[5,5,196...) while((s32[]{:T(128)}, f32[14,14,64]{2,1,0:T(8,128)S(1)}, ...), condition=%wide.region_18.19_spmd.clone, body=%wide.region_16.18_spmd.clone.sunk | while | flops 741679872 | bytes 70086392 | solution.py:294
  821.9 3.4 multiply_reduce_fusion.6
  866.7 3.4 multiply_reduce_fusion.6
  911.4 3.4 multiply_reduce_fusion.6
  956.2 3.4 multiply_reduce_fusion.6
  1000.9 3.4 multiply_reduce_fusion.6
  1034.8 20.7 %copy.171 = bf16[5,5,196,3,3,64]{5,4,3,2,1,0:T(4,128)(2,1)} copy(bf16[5,5,196,3,3,64]{2,5,4,1,3,0:T(8,128)(2,1)} %get-tuple-element.171) | data formatting | bytes 11289600 | tf_op jit(solution)/shard_map/while | solution.py:294
  1055.5 26.6 %reshape_reshape.15 = bf16[1,5,5,14,14,576]{5,4,3,2,1,0:T(8,128)(2,1)} reshape(bf16[5,5,196,3,3,64]{5,4,3,2,1,0:T(4,128)(2,1)} %copy.171) | data formatting | bytes 11289600 | tf_op jit(solution)/shard_map/reshape;reshape | solution.py:50
  1082.1 6.5 copy.172
  1088.6 10.7 reshape.279
  1104.6 6.9 convolution_convert_fusion
  1112.8 8.0 copy.173
  1120.8 6.4 fusion.249
  1127.3 9.7 fusion.182
  1137.1 4.5 convert_reduce_fusion.1
  1141.8 22.4 %all-reduce.3 = (f32[2,192]{1,0:T(2,128)}, f32[768]{0:T(1024)}) all-reduce(f32[2,192]{1,0:T(2,128)S(1)} %pad_maximum_fusion.3, f32[768]{0:T(1024)S(1)} %copy-done.35), channel_id=1, replica_groups=mesh['dp'=8,'tensor'=4] {'dp'}, use_global_device_ids=true, to_apply=%region_28.29 | all-reduce | flops 1152 | bytes 9216 | tf_op jit(solution)/shard_map/psum | solution.py:342
  1164.9 5.2 reduce-scatter.15.cloned.1.call-done
  1173.2 41.7 %all-reduce.2 = (f32[768]{0:T(1024)}, f32[768]{0:T(1024)}, f32[27,64]{1,0:T(8,128)}, f32[27,64]{1,0:T(8,128)}, f32[768]{0:T(1024)}, /*index=5*/f32[768]{0:T(1024)}, f32[768]{0:T(1024)}, f32[768]{0:T(1024)}) all-reduce(f32[768]{0:T(1024)S(1)} %get-tuple-element.320, ...), channel_id=1, replica_groups=mesh['dp'=8,'tensor'=4] {'dp','tensor'}, use_global_device_ids=true, to_apply=%region_23.24 | all-reduce | flops 8064 | bytes 64512 | tf_op jit(solution)/shard_map/psum | solution.py:329
  1215.0 3.6 fusion.199
  1218.6 25.1 %reduce-scatter.21.cloned.1.call-done = f32[96,768]{1,0:T(8,128)} async-done(((f32[768,768]{1,0:T(8,128)}), f32[96,768]{1,0:T(8,128)}) %reduce-scatter.21.cloned.1.call-update) | async-done | bytes 294928 | tf_op jit(solution)/shard_map/reduce_scatter | solution.py:317
  1243.8 72.0 %reduce-scatter.23.cloned.1.call-done = f32[96,768]{1,0:T(8,128)} async-done(((f32[768,768]{1,0:T(8,128)}), f32[96,768]{1,0:T(8,128)}) %reduce-scatter.23.cloned.1.call-update) | async-done | bytes 294928 | tf_op jit(solution)/shard_map/reduce_scatter | solution.py:318
  1315.8 65.4 %reduce-scatter.19.cloned.1.call-done = f32[96,192]{1,0:T(8,128)} async-done(((f32[768,192]{1,0:T(8,128)}), f32[96,192]{1,0:T(8,128)}) %reduce-scatter.19.cloned.1.call-update) | async-done | bytes 73744 | tf_op jit(solution)/shard_map/reduce_scatter | solution.py:316
  1381.1 72.4 %reduce-scatter.17.cloned.1.call-done = f32[96,3,192]{2,0,1:T(8,128)} async-done(((f32[768,3,192]{2,0,1:T(8,128)}), f32[96,3,192]{2,0,1:T(8,128)}) %reduce-scatter.17.cloned.1.call-update) | async-done | bytes 221200 | tf_op jit(solution)/shard_map/reduce_scatter | solution.py:315
  (560 shorter events, 337.8 us)
Async XLA Ops:
  8.0 80.5 %copy-start = (bf16[27,64]{1,0:T(8,128)(2,1)S(1)}, bf16[27,64]{1,0:T(8,128)(2,1)}, u32[]{:S(2)}) copy-start(bf16[27,64]{1,0:T(8,128)(2,1)} %param.28) | copy-start | bytes 10372
  8.1 80.9 %all-gather.6.cloned.1.call-start = ((), (), s32[]{:S(2)}) async-start(), calls=%async_computation.8 | async-start | bytes 7864320 | tf_op jit(solution)/shard_map/all_gather | solution.py:222
  14.4 41.0 %copy-start.49 = (bf16[96,192]{1,0:T(8,128)(2,1)S(1)}, bf16[96,192]{1,0:T(8,128)(2,1)}, u32[]{:S(2)}) copy-start(bf16[96,192]{1,0:T(8,128)(2,1)} %param.29) | copy-start | bytes 110596
  14.4 74.3 %copy-start.65 = (bf16[27,64]{1,0:T(8,128)(2,1)S(1)}, bf16[27,64]{1,0:T(8,128)(2,1)}, u32[]{:S(2)}) copy-start(bf16[27,64]{1,0:T(8,128)(2,1)} %param.27) | copy-start | bytes 10372
  14.4 342.4 %reduce-scatter.9.cloned.1.call-start = ((), (), s32[]{:S(2)}) async-start(), calls=%async_computation.9 | async-start | bytes 15728640 | tf_op jit(solution)/shard_map/reduce_scatter | solution.py:247
  54.6 72.3 %copy-start.29 = (bf16[768,3,192]{0,2,1:T(8,128)(2,1)}, bf16[768,3,192]{0,2,1:T(8,128)(2,1)S(1)}, u32[]{:S(2)}) copy-start(bf16[768,3,192]{0,2,1:T(8,128)(2,1)S(1)} %copy.163) | copy-start | bytes 2654212
  54.7 40.8 %copy-start.43 = (s32[14,14]{1,0:T(8,128)}, s32[14,14]{1,0:T(8,128)S(1)}, u32[]{:S(2)}) copy-start(s32[14,14]{1,0:T(8,128)S(1)} %subtract_add_fusion) | copy-start | bytes 2356
  226.2 8.9 copy-start.19
  226.2 8.9 copy-start.21
  226.2 8.9 copy-start.26
  258.2 199.3 %all-gather.8.cloned.1.call-start = ((), (), s32[]{:S(2)}) async-start(), calls=%async_computation.10 | async-start | bytes 1327104 | tf_op jit(solution)/shard_map/all_gather | solution.py:211
  258.8 198.7 %all-gather.10.cloned.1.call-start = ((), (), s32[]{:S(2)}) async-start(), calls=%async_computation.11 | async-start | bytes 1327104 | tf_op jit(solution)/shard_map/all_gather | solution.py:212
  259.4 198.2 %all-gather.12.cloned.1.call-start = ((), (), s32[]{:S(2)}) async-start(), calls=%async_computation.13 | async-start | bytes 7864320 | tf_op jit(solution)/shard_map/all_gather | solution.py:269
  259.9 408.6 %reduce-scatter.13.cloned.1.call-start = ((), (), s32[]{:S(2)}) async-start(), calls=%async_computation.14 | async-start | bytes 15728640 | tf_op jit(solution)/shard_map/reduce_scatter | solution.py:273
  260.0 193.9 %copy-start.37 = (f32[768]{0:T(1024)}, f32[768]{0:T(1024)S(1)}, u32[]{:S(2)}) copy-start(f32[768]{0:T(1024)S(1)} %convert_element_type.146) | copy-start | bytes 9220
  359.6 94.3 %copy-start.10 = (f32[1024,768]{1,0:T(8,128)}, f32[1024,768]{1,0:T(8,128)S(1)}, u32[]{:S(2)}) copy-start(f32[1024,768]{1,0:T(8,128)S(1)} %get-tuple-element.398) | copy-start | bytes 9437188
  359.7 94.3 %copy-start.32 = (f32[1024]{0:T(1024)}, f32[1024]{0:T(1024)S(1)}, u32[]{:S(2)}) copy-start(f32[1024]{0:T(1024)S(1)} %broadcast_multiply_fusion.4) | copy-start | bytes 12292
  360.2 66.8 %copy-start.60 = (bf16[768]{0:T(1024)(128)(2,1)S(1)}, bf16[768]{0:T(1024)(128)(2,1)}, u32[]{:S(2)}) copy-start(bf16[768]{0:T(1024)(128)(2,1)} %param.34) | copy-start | bytes 4612
  360.2 93.7 %copy-start.39 = (f32[1024]{0:T(1024)}, f32[1024]{0:T(1024)S(1)}, u32[]{:S(2)}) copy-start(f32[1024]{0:T(1024)S(1)} %add_rsqrt_fusion) | copy-start | bytes 12292
  360.8 44.6 %collective-permute-start = (bf16[1024,768]{1,0:T(8,128)(2,1)S(1)}, bf16[1024,768]{1,0:T(8,128)(2,1)S(1)}, u32[]{:S(2)}, u32[]{:S(2)}) collective-permute-start(bf16[1024,768]{1,0:T(8,128)(2,1)S(1)} %add_convert_fusion.2), channel_id=1, source_target_pairs={{0,1},{1,2},{2,3},{3,0},{4,5},{5,6},{6,7},{7,4},{8,9},{9,10},{10,1... | collective-permute-start | bytes 4718600 | tf_op jit(solution)/shard_map/ppermute | solution.py:259
  406.6 19.9 %collective-permute-start.1 = (bf16[1024,768]{1,0:T(8,128)(2,1)S(1)}, bf16[1024,768]{1,0:T(8,128)(2,1)}, u32[]{:S(2)}, u32[]{:S(2)}) collective-permute-start(bf16[1024,768]{1,0:T(8,128)(2,1)S(1)} %collective-permute-done), channel_id=1, source_target_pairs={{0,1},{1,2},{2,3},{3,0},{4,5},{5,6},{6,7},{7,4},{8,9},{9,10},{10,1... | collective-permute-start | bytes 4718600 | tf_op jit(solution)/shard_map/ppermute | solution.py:259
  426.5 20.5 %collective-permute-start.2 = (bf16[1024,768]{1,0:T(8,128)(2,1)}, bf16[1024,768]{1,0:T(8,128)(2,1)}, u32[]{:S(2)}, u32[]{:S(2)}) collective-permute-start(bf16[1024,768]{1,0:T(8,128)(2,1)} %collective-permute-done.1), channel_id=1, source_target_pairs={{0,1},{1,2},{2,3},{3,0},{4,5},{5,6},{6,7},{7,4},{8,9},{9,10},{10,1... | collective-permute-start | bytes 4718600 | tf_op jit(solution)/shard_map/ppermute | solution.py:259
  427.0 23.1 %copy-start.25 = (bf16[1024,768]{1,0:T(8,128)(2,1)S(1)}, bf16[1024,768]{1,0:T(8,128)(2,1)}, u32[]{:S(2)}) copy-start(bf16[1024,768]{1,0:T(8,128)(2,1)} %copy-done.24) | copy-start | bytes 4718596
  460.8 5.4 copy-start.66
  485.5 5.4 copy-start.66
  492.2 5.2 copy-start.67
  511.2 5.4 copy-start.66
  517.8 5.2 copy-start.67
  536.8 5.4 copy-start.66
  543.5 5.2 copy-start.67
  559.3 10.2 copy-start.34
  569.5 159.9 %reduce-scatter.11.cloned.1.call-start = ((), (), s32[]{:S(2)}) async-start(), calls=%async_computation.12 | async-start | bytes 7864320 | tf_op jit(solution)/shard_map/reduce_scatter | solution.py:263
  608.9 59.6 %copy-start.11 = (f32[1024,768]{1,0:T(8,128)S(1)}, f32[1024,768]{1,0:T(8,128)}, u32[]{:S(2)}) copy-start(f32[1024,768]{1,0:T(8,128)} %copy-done.10) | copy-start | bytes 9437188
  608.9 59.6 %copy-start.33 = (f32[1024]{0:T(1024)S(1)}, f32[1024]{0:T(1024)}, u32[]{:S(2)}) copy-start(f32[1024]{0:T(1024)} %copy-done.32) | copy-start | bytes 12292
  608.9 59.6 %copy-start.38 = (f32[768]{0:T(1024)S(1)}, f32[768]{0:T(1024)}, u32[]{:S(2)}) copy-start(f32[768]{0:T(1024)} %copy-done.37) | copy-start | bytes 9220
  608.9 59.6 %copy-start.40 = (f32[1024]{0:T(1024)S(1)}, f32[1024]{0:T(1024)}, u32[]{:S(2)}) copy-start(f32[1024]{0:T(1024)} %copy-done.39) | copy-start | bytes 12292
  609.0 173.0 %all-gather.14.cloned.1.call-start = ((), (), s32[]{:S(2)}) async-start(), calls=%async_computation.15 | async-start | bytes 7864320 | tf_op jit(solution)/shard_map/all_gather | solution.py:285
  735.5 434.7 %reduce-scatter.15.cloned.1.call-start = ((), (), s32[]{:S(2)}) async-start(), calls=%async_computation.16 | async-start | bytes 7864320 | tf_op jit(solution)/shard_map/reduce_scatter | solution.py:302
  802.1 8.5 copy-start.20
  802.1 8.5 copy-start.22
  802.1 8.5 copy-start.27
  802.1 8.5 copy-start.31
  812.5 8.1 copy-start.9
  857.2 8.1 copy-start.9
  902.0 8.1 copy-start.9
  946.7 8.1 copy-start.9
  991.4 8.1 copy-start.9
  1099.3 5.3 copy-start.30
  1111.6 132.1 %reduce-scatter.21.cloned.1.call-start = ((), (), s32[]{:S(2)}) async-start(), calls=%async_computation.19 | async-start | bytes 2654208 | tf_op jit(solution)/shard_map/reduce_scatter | solution.py:317
  1112.2 203.6 %reduce-scatter.23.cloned.1.call-start = ((), (), s32[]{:S(2)}) async-start(), calls=%async_computation.20 | async-start | bytes 2654208 | tf_op jit(solution)/shard_map/reduce_scatter | solution.py:318
  1112.8 268.4 %reduce-scatter.19.cloned.1.call-start = ((), (), s32[]{:S(2)}) async-start(), calls=%async_computation.18 | async-start | bytes 884736 | tf_op jit(solution)/shard_map/reduce_scatter | solution.py:316
  1112.8 8.0 copy-start.17
  1127.2 326.3 %reduce-scatter.17.cloned.1.call-start = ((), (), s32[]{:S(2)}) async-start(), calls=%async_computation.17 | async-start | bytes 2654208 | tf_op jit(solution)/shard_map/reduce_scatter | solution.py:315
  1137.0 27.2 %copy-start.44 = (s32[14,14]{1,0:T(8,128)S(1)}, s32[14,14]{1,0:T(8,128)}, u32[]{:S(2)}) copy-start(s32[14,14]{1,0:T(8,128)} %copy-done.43) | copy-start | bytes 2356
  1137.0 33.1 %copy-start.15 = (bf16[1024,768]{1,0:T(8,128)(2,1)S(1)}, bf16[1024,768]{1,0:T(8,128)(2,1)}, u32[]{:S(2)}) copy-start(bf16[1024,768]{1,0:T(8,128)(2,1)} %param.22) | copy-start | bytes 4718596
  1137.0 33.1 %copy-start.42 = (f32[1024]{0:T(1024)S(1)}, f32[1024]{0:T(1024)}, u32[]{:S(2)}) copy-start(f32[1024]{0:T(1024)} %copy-done.41) | copy-start | bytes 12292
  1137.0 33.1 %copy-start.46 = (f32[1024]{0:T(1024)S(1)}, f32[1024]{0:T(1024)}, u32[]{:S(2)}) copy-start(f32[1024]{0:T(1024)} %copy-done.45) | copy-start | bytes 12292
  1137.0 33.1 %copy-start.48 = (f32[768]{0:T(1024)S(1)}, f32[768]{0:T(1024)}, u32[]{:S(2)}) copy-start(f32[768]{0:T(1024)} %copy-done.47) | copy-start | bytes 9220
  1141.5 31.7 %copy-start.50 = (f32[768]{0:T(1024)S(1)}, f32[768]{0:T(1024)}, u32[]{:S(2)}) copy-start(f32[768]{0:T(1024)} %get-tuple-element.318) | copy-start | bytes 9220
  1141.5 31.7 %copy-start.51 = (f32[768]{0:T(1024)S(1)}, f32[768]{0:T(1024)}, u32[]{:S(2)}) copy-start(f32[768]{0:T(1024)} %get-tuple-element.323) | copy-start | bytes 9220
  1141.5 31.7 %copy-start.52 = (f32[768]{0:T(1024)S(1)}, f32[768]{0:T(1024)}, u32[]{:S(2)}) copy-start(f32[768]{0:T(1024)} %get-tuple-element.394) | copy-start | bytes 9220
  1141.6 31.7 %copy-start.53 = (f32[768]{0:T(1024)S(1)}, f32[768]{0:T(1024)}, u32[]{:S(2)}) copy-start(f32[768]{0:T(1024)} %get-tuple-element.408) | copy-start | bytes 9220
  1170.1 44.8 %copy-start.23 = (bf16[1024,768]{1,0:T(8,128)(2,1)S(1)}, bf16[1024,768]{1,0:T(8,128)(2,1)}, u32[]{:S(2)}) copy-start(bf16[1024,768]{1,0:T(8,128)(2,1)} %reduce-scatter.15.cloned.1.call-done) | copy-start | bytes 4718596
  1215.0 238.6 %copy-start.1 = (bf16[27,64]{1,0:T(8,128)(2,1)S(1)}, bf16[27,64]{1,0:T(8,128)(2,1)}, u32[]{:S(2)}) copy-start(bf16[27,64]{1,0:T(8,128)(2,1)} %param.28) | copy-start | bytes 10372
  (69 other events, 170.2 us)
Sparse Core Ops, SparseCore 0:
  14.6 49.0 all-gather.5
  258.3 98.4 reduce-scatter.8
  735.6 46.3 all-gather.13
  1111.7 58.3 reduce-scatter.14
  1174.0 69.6 reduce-scatter.20
  1247.7 68.0 reduce-scatter.22
  1319.7 61.4 reduce-scatter.18
  1385.6 67.8 reduce-scatter.16
Sparse Core Ops, SparseCore 1:
  260.8 40.6 all-gather.7
  303.6 40.0 all-gather.9
  345.1 57.5 all-gather.11
  569.6 98.9 reduce-scatter.12
  671.1 58.2 reduce-scatter.10
